TPU v7x, 256 devices: a whole 4x4x8 slice. The times are simulated.
256 devices in a mesh: seq: 32 (over x, z), head: 8 (over y, core).
Axes of the slice: x: 4, y: 4, z: 8, core: 2. Of those that a mesh axis runs over, the one named last changes fastest.
Arguments:
- tokens: bfloat16 [8192, 3072], P('seq', 'head'), may hold values from -6 to 6
- norm_gain: float32 [3072], replicated, may hold values from 0.1 to 1.9
- w_query: bfloat16 [3072, 3072], P(None, 'head'), may hold values from -0.109375 to 0.109375
- w_key: bfloat16 [3072, 1024], P(None, 'head'), may hold values from -0.3125 to 0.3125
- w_value: bfloat16 [3072, 1024], P(None, 'head'), may hold values from -0.109375 to 0.109375
- w_out: bfloat16 [3072, 3072], P('head'), may hold values from -0.109375 to 0.109375
- keys_cache: bfloat16 [65536, 1024], P('seq', 'head'), may hold values from -120 to 120
- values_cache: bfloat16 [65536, 1024], P('seq', 'head'), may hold values from -6 to 6
- cached_lengths: int32 [4], replicated, may hold values from 0 to 14336, as said below
- rope_offsets: int32 [4], replicated, may hold values from 0 to 8191
Outputs:
- attn_proj: bfloat16 [8192, 3072], P('seq', 'head')
- keys_updated: bfloat16 [65536, 1024], P('seq', 'head')
- values_updated: bfloat16 [65536, 1024], P('seq', 'head')
Inputs may be any that keep to these rules, and one draw needn't show every extreme that they name: `cached_lengths`: in every draw one request has exactly 14336 cached tokens.
All inputs are finite; a program needn't handle non-finite values.
Results may differ from a plain program's by a relative error of at most 0.02.
Values may be sent and summed in bfloat16 or wider, within the bound.
A program may use at most 128 MiB of HBM per device.

v0:
```python
import math
import jax
import jax.numpy as jnp
from jax import lax
from jax.sharding import PartitionSpec as P

HD = 128
rope_base = 500000.0
neg_large = -1e30


def shifted(shard, axis, by):
    devices = lax.axis_size(axis)
    return lax.ppermute(shard, axis, [(i, (i + by) % devices) for i in range(devices)])


def rotate(vectors, positions):
    half_width = vectors.shape[-1] // 2
    frequency = rope_base ** (-jnp.arange(half_width, dtype=jnp.float32) * 2.0 / vectors.shape[-1])
    angles = positions.astype(jnp.float32)[:, None] * frequency[None, :]
    cosine = jnp.cos(angles)[:, None, :]
    sine_part = jnp.sin(angles)[:, None, :]
    first_half = vectors[..., :half_width]
    second_half = vectors[..., half_width:]
    return jnp.concatenate(
        [
            first_half * cosine - second_half * sine_part,
            second_half * cosine + first_half * sine_part,
        ],
        -1,
    )


def shards(
    tokens,
    norm_gain,
    w_query,
    w_key,
    w_value,
    w_out,
    keys_cache,
    values_cache,
    cached_lengths,
    rope_offsets,
):
    gathered = lax.all_gather(tokens, "head", axis=1, tiled=True)
    row_count = gathered.shape[0]
    requests = cached_lengths.shape[0]
    groups = lax.axis_size("seq") // requests
    member = lax.axis_index("seq")
    request = member % requests
    position_in = member // requests
    length = lax.dynamic_index_in_dim(cached_lengths, request, 0, False)
    offset = lax.dynamic_index_in_dim(rope_offsets, request, 0, False)
    widened = gathered.astype(jnp.float32)
    normed = (
        widened * lax.rsqrt(jnp.mean(widened * widened, -1, keepdims=True) + 1e-05) * norm_gain
    ).astype(jnp.bfloat16)
    index_new = position_in * row_count + jnp.arange(row_count, dtype=jnp.int32)
    positions = offset + length + index_new
    kv_heads = w_key.shape[1] // HD
    q_heads = w_query.shape[1] // HD
    repeat = q_heads // kv_heads
    queries = rotate(
        jnp.dot(normed, w_query, preferred_element_type=jnp.float32).reshape(
            row_count, q_heads, HD
        ),
        positions,
    ).astype(jnp.bfloat16)
    new_keys = (
        rotate(
            jnp.dot(normed, w_key, preferred_element_type=jnp.float32).reshape(
                row_count, kv_heads, HD
            ),
            positions,
        )
        .astype(jnp.bfloat16)
        .reshape(row_count, kv_heads * HD)
    )
    new_values = jnp.dot(normed, w_value, preferred_element_type=jnp.float32).astype(jnp.bfloat16)
    grouped = (
        queries.reshape(row_count, kv_heads, repeat, HD)
        .transpose(1, 2, 0, 3)
        .reshape(kv_heads, repeat * row_count, HD)
    )
    slab_rows = keys_cache.shape[0]
    score_scale = 1.0 / math.sqrt(HD)

    def attend(softmax_state, query_group, key_block, value_block, visible):
        running_max, denominator, accumulated = softmax_state
        scores = (
            jnp.einsum(
                "gqd,kgd->gqk",
                query_group,
                key_block.reshape(-1, kv_heads, HD),
                preferred_element_type=jnp.float32,
            )
            * score_scale
        )
        masked = jnp.where(visible, scores, neg_large)
        new_max = jnp.maximum(running_max, jnp.max(masked, -1))
        weights = jnp.where(visible, jnp.exp(masked - new_max[..., None]), 0.0)
        factor = jnp.exp(running_max - new_max)
        denominator = denominator * factor + jnp.sum(weights, -1)
        accumulated = accumulated * factor[..., None] + jnp.einsum(
            "gqk,kgd->gqd",
            weights.astype(jnp.bfloat16),
            value_block.reshape(-1, kv_heads, HD),
            preferred_element_type=jnp.float32,
        )
        return (new_max, denominator, accumulated)

    def attend_pair(
        softmax_state,
        query_anchor,
        query_group,
        slab_keys,
        slab_values,
        slab_source,
        fresh_keys,
        fresh_values,
        fresh_source,
    ):
        query_index = jnp.tile(
            query_anchor * row_count + jnp.arange(row_count, dtype=jnp.int32), repeat
        )
        slots = slab_source * slab_rows + jnp.arange(slab_rows, dtype=jnp.int32)
        old_visible = (slots < length)[None, None, :]
        fresh_index = fresh_source * row_count + jnp.arange(row_count, dtype=jnp.int32)
        fresh_visible = (fresh_index[None, :] <= query_index[:, None])[None]
        softmax_state = attend(softmax_state, query_group, slab_keys, slab_values, old_visible)
        softmax_state = attend(softmax_state, query_group, fresh_keys, fresh_values, fresh_visible)
        return softmax_state

    def write_fresh(out_keys, out_values, fresh_keys, fresh_values, fresh_source):
        fresh_index = fresh_source * row_count + jnp.arange(row_count, dtype=jnp.int32)
        local_slot = length + fresh_index - position_in * slab_rows
        target = jnp.where((local_slot >= 0) & (local_slot < slab_rows), local_slot, slab_rows)
        out_keys = out_keys.at[target].set(fresh_keys, mode="drop")
        out_values = out_values.at[target].set(fresh_values, mode="drop")
        return (out_keys, out_values)

    def absorb(loop_carry, incoming, source):
        softmax_state, out_keys, out_values = loop_carry
        fresh_keys = incoming[0, slab_rows:]
        fresh_values = incoming[1, slab_rows:]
        softmax_state = attend_pair(
            softmax_state,
            position_in,
            grouped,
            incoming[0, :slab_rows],
            incoming[1, :slab_rows],
            source,
            fresh_keys,
            fresh_values,
            source,
        )
        out_keys, out_values = write_fresh(out_keys, out_values, fresh_keys, fresh_values, source)
        return (softmax_state, out_keys, out_values)

    start_state = (
        jnp.full((kv_heads, repeat * row_count), neg_large, jnp.float32),
        jnp.zeros((kv_heads, repeat * row_count), jnp.float32),
        jnp.zeros((kv_heads, repeat * row_count, HD), jnp.float32),
    )
    outgoing = jnp.stack(
        [
            jnp.concatenate([keys_cache, new_keys], 0),
            jnp.concatenate([values_cache, new_values], 0),
        ],
        0,
    )
    loop_carry = absorb((start_state, keys_cache, values_cache), outgoing, position_in)

    def cycle_step(cycle_turn, cycle_carry):
        held_blocks, inner_carry = cycle_carry
        held_blocks = shifted(held_blocks, "seq", requests)
        source = (position_in - cycle_turn) % groups
        return (held_blocks, absorb(inner_carry, held_blocks, source))

    unused, loop_carry = lax.fori_loop(1, groups, cycle_step, (outgoing, loop_carry))
    final_state, keys_updated, values_updated = loop_carry
    running_max, denominator, accumulated = final_state
    attended = (
        (accumulated / denominator[..., None])
        .reshape(kv_heads, repeat, row_count, HD)
        .transpose(2, 0, 1, 3)
        .reshape(row_count, q_heads * HD)
        .astype(jnp.bfloat16)
    )
    partial_value = jnp.dot(attended, w_out, preferred_element_type=jnp.float32)
    summed = lax.psum(partial_value.astype(jnp.bfloat16), "head").astype(jnp.float32)
    share_width = partial_value.shape[1] // lax.axis_size("head")
    projected = lax.dynamic_slice_in_dim(
        summed, lax.axis_index("head") * share_width, share_width, 1
    )
    return (projected.astype(jnp.bfloat16), keys_updated, values_updated)


def solution(mesh):
    return jax.shard_map(
        shards,
        mesh=mesh,
        in_specs=(
            P("seq", "head"),
            P(),
            P(None, "head"),
            P(None, "head"),
            P(None, "head"),
            P("head", None),
            P("seq", "head"),
            P("seq", "head"),
            P(),
            P(),
        ),
        out_specs=(P("seq", "head"), P("seq", "head"), P("seq", "head")),
        check_vma=False,
    )
```

profile of v0, /device:TPU:2, one launch (start us, length us, event | category | flops | bytes accessed | tf_op | source)
XLA Modules:
  0.0 639.8 jit_solution(14705658243390205139)
XLA Ops:
  17.2 23.6 %all-gather.2.cloned.1.call-done = bf16[256,3072]{1,0:T(8,128)(2,1)} async-done(((bf16[256,384]{1,0:T(8,128)(2,1)}), bf16[256,3072]{1,0:T(8,128)(2,1)}) %all-gather.2.cloned.1.call-update) | async-done | bytes 1572880 | tf_op jit(solution)/shard_map/all_gather | solution.py:46
  49.5 3.2 scatter_custom_fusion.2
  53.9 3.2 scatter_custom_fusion.3
  57.1 3.3 fusion.81
  71.4 386.1 %while.25 = (s32[]{:T(128)}, bf16[2,2304,128]{2,1,0:T(8,128)(2,1)}, f32[1,768]{1,0:T(1,128)S(1)}, f32[1,768]{1,0:T(1,128)}, f32[1,768,128]{2,1,0:T(8,128)}, /*in...) while((s32[]{:T(128)}, bf16[2,2304,128]{2,1,0:T(8,128)(2,1)}, ...), condition=%wide.region_14.15_spmd, body=%wide.region_7.14_spmd.sunk | while | flops 929181184 | bytes 57951692 | solution.py:181
  71.4 5.7 collective-permute-start
  79.0 41.7 %collective-permute-done = bf16[2,2304,128]{2,1,0:T(8,128)(2,1)S(1)} collective-permute-done((bf16[2,2304,128]{2,1,0:T(8,128)(2,1)}, bf16[2,2304,128]{2,1,0:T(8,128)(2,1)S(1)}, u32[]{:S(2)}, u32[]{:S(2)}) %collective-permute-start) | collective-permute-done | bytes 1179680 | tf_op jit(solution)/shard_map/while/body/eval_jaxpr/ppermute | solution.py:14
  129.5 3.2 scatter_custom_fusion.14
  132.7 3.2 scatter_custom_fusion.15
  135.8 5.2 fusion.109
  141.0 5.1 collective-permute-start
  148.0 23.2 %collective-permute-done = bf16[2,2304,128]{2,1,0:T(8,128)(2,1)S(1)} collective-permute-done((bf16[2,2304,128]{2,1,0:T(8,128)(2,1)}, bf16[2,2304,128]{2,1,0:T(8,128)(2,1)S(1)}, u32[]{:S(2)}, u32[]{:S(2)}) %collective-permute-start) | collective-permute-done | bytes 1179680 | tf_op jit(solution)/shard_map/while/body/eval_jaxpr/ppermute | solution.py:14
  180.0 3.2 scatter_custom_fusion.14
  183.2 3.2 scatter_custom_fusion.15
  186.4 5.2 fusion.109
  191.5 4.2 collective-permute-start
  197.6 27.7 %collective-permute-done = bf16[2,2304,128]{2,1,0:T(8,128)(2,1)S(1)} collective-permute-done((bf16[2,2304,128]{2,1,0:T(8,128)(2,1)}, bf16[2,2304,128]{2,1,0:T(8,128)(2,1)S(1)}, u32[]{:S(2)}, u32[]{:S(2)}) %collective-permute-start) | collective-permute-done | bytes 1179680 | tf_op jit(solution)/shard_map/while/body/eval_jaxpr/ppermute | solution.py:14
  234.1 3.2 scatter_custom_fusion.14
  237.3 3.2 scatter_custom_fusion.15
  240.5 5.2 fusion.109
  249.1 29.3 %collective-permute-done = bf16[2,2304,128]{2,1,0:T(8,128)(2,1)S(1)} collective-permute-done((bf16[2,2304,128]{2,1,0:T(8,128)(2,1)}, bf16[2,2304,128]{2,1,0:T(8,128)(2,1)S(1)}, u32[]{:S(2)}, u32[]{:S(2)}) %collective-permute-start) | collective-permute-done | bytes 1179680 | tf_op jit(solution)/shard_map/while/body/eval_jaxpr/ppermute | solution.py:14
  287.2 3.2 scatter_custom_fusion.14
  293.6 5.2 fusion.109
  303.4 27.8 %collective-permute-done = bf16[2,2304,128]{2,1,0:T(8,128)(2,1)S(1)} collective-permute-done((bf16[2,2304,128]{2,1,0:T(8,128)(2,1)}, bf16[2,2304,128]{2,1,0:T(8,128)(2,1)S(1)}, u32[]{:S(2)}, u32[]{:S(2)}) %collective-permute-start) | collective-permute-done | bytes 1179680 | tf_op jit(solution)/shard_map/while/body/eval_jaxpr/ppermute | solution.py:14
  340.0 3.2 scatter_custom_fusion.14
  346.4 5.2 fusion.109
  351.5 3.2 collective-permute-start
  356.7 27.8 %collective-permute-done = bf16[2,2304,128]{2,1,0:T(8,128)(2,1)S(1)} collective-permute-done((bf16[2,2304,128]{2,1,0:T(8,128)(2,1)}, bf16[2,2304,128]{2,1,0:T(8,128)(2,1)S(1)}, u32[]{:S(2)}, u32[]{:S(2)}) %collective-permute-start) | collective-permute-done | bytes 1179680 | tf_op jit(solution)/shard_map/while/body/eval_jaxpr/ppermute | solution.py:14
  399.7 5.2 fusion.109
  409.3 27.8 %collective-permute-done = bf16[2,2304,128]{2,1,0:T(8,128)(2,1)S(1)} collective-permute-done((bf16[2,2304,128]{2,1,0:T(8,128)(2,1)}, bf16[2,2304,128]{2,1,0:T(8,128)(2,1)S(1)}, u32[]{:S(2)}, u32[]{:S(2)}) %collective-permute-start) | collective-permute-done | bytes 1179680 | tf_op jit(solution)/shard_map/while/body/eval_jaxpr/ppermute | solution.py:14
  452.3 5.2 fusion.109
  461.7 169.6 %all-reduce.2.cloned.1.call-done = bf16[256,3072]{1,0:T(8,128)(2,1)} async-done(((bf16[256,3072]{1,0:T(8,128)(2,1)}), bf16[256,3072]{1,0:T(8,128)(2,1)}) %all-reduce.2.cloned.1.call-update) | async-done | bytes 1572880 | tf_op jit(solution)/shard_map/psum | solution.py:192
  (211 shorter events, 135.5 us)
Async XLA Ops:
  7.2 452.3 %copy-start = (bf16[384,3072]{1,0:T(8,128)(2,1)S(1)}, bf16[384,3072]{1,0:T(8,128)(2,1)}, u32[]{:S(2)}) copy-start(bf16[384,3072]{1,0:T(8,128)(2,1)} %param.17) | copy-start | bytes 7077892
  7.2 36.1 %copy-start.9 = (f32[3072]{0:T(1024)S(1)}, f32[3072]{0:T(1024)}, u32[]{:S(2)}) copy-start(f32[3072]{0:T(1024)} %param.13) | copy-start | bytes 36868
  7.2 33.6 %all-gather.2.cloned.1.call-start = ((), (), s32[]{:S(2)}) async-start(), calls=%async_computation | async-start | bytes 1769472 | tf_op jit(solution)/shard_map/all_gather | solution.py:46
  8.4 37.7 %copy-start.2 = (bf16[2048,128]{1,0:T(8,128)(2,1)}, bf16[2048,128]{1,0:T(8,128)(2,1)S(1)}, u32[]{:S(2)}) copy-start(bf16[2048,128]{1,0:T(8,128)(2,1)S(1)} %copy.52) | copy-start | bytes 1572868
  10.5 620.8 %all-reduce.2.cloned.1.call-start = ((), (), s32[]{:S(2)}) async-start(), calls=%async_computation.1 | async-start | bytes 3145728 | tf_op jit(solution)/shard_map/psum | solution.py:192
  48.4 8.6 %copy-start.8 = (f32[256]{0:T(256)S(1)}, f32[256]{0:T(256)}, u32[]{:S(2)}) copy-start(f32[256]{0:T(256)} %copy-done.7) | copy-start | bytes 3076
  57.1 3.4 copy-start.3
  57.1 3.4 copy-start.4
  71.4 49.3 %collective-permute-start = (bf16[2,2304,128]{2,1,0:T(8,128)(2,1)}, bf16[2,2304,128]{2,1,0:T(8,128)(2,1)S(1)}, u32[]{:S(2)}, u32[]{:S(2)}) collective-permute-start(bf16[2,2304,128]{2,1,0:T(8,128)(2,1)} %get-tuple-element.428), channel_id=1, source_target_pairs={{0,32},{8,40},{16,48},{24,56},{32,64},{40,72},{48,80},{56,88},{64,... | collective-permute-start | bytes 3538952 | tf_op jit(solution)/shard_map/while/body/eval_jaxpr/ppermute | solution.py:14
  122.8 4.2 copy-start.1
  125.4 1.8 copy-start.5
  127.3 1.2 copy-start.6
  141.0 30.2 %collective-permute-start = (bf16[2,2304,128]{2,1,0:T(8,128)(2,1)}, bf16[2,2304,128]{2,1,0:T(8,128)(2,1)S(1)}, u32[]{:S(2)}, u32[]{:S(2)}) collective-permute-start(bf16[2,2304,128]{2,1,0:T(8,128)(2,1)} %get-tuple-element.428), channel_id=1, source_target_pairs={{0,32},{8,40},{16,48},{24,56},{32,64},{40,72},{48,80},{56,88},{64,... | collective-permute-start | bytes 3538952 | tf_op jit(solution)/shard_map/while/body/eval_jaxpr/ppermute | solution.py:14
  173.3 4.2 copy-start.1
  175.9 1.8 copy-start.5
  191.5 33.8 %collective-permute-start = (bf16[2,2304,128]{2,1,0:T(8,128)(2,1)}, bf16[2,2304,128]{2,1,0:T(8,128)(2,1)S(1)}, u32[]{:S(2)}, u32[]{:S(2)}) collective-permute-start(bf16[2,2304,128]{2,1,0:T(8,128)(2,1)} %get-tuple-element.428), channel_id=1, source_target_pairs={{0,32},{8,40},{16,48},{24,56},{32,64},{40,72},{48,80},{56,88},{64,... | collective-permute-start | bytes 3538952 | tf_op jit(solution)/shard_map/while/body/eval_jaxpr/ppermute | solution.py:14
  227.4 4.2 copy-start.1
  230.1 1.8 copy-start.5
  245.7 32.8 %collective-permute-start = (bf16[2,2304,128]{2,1,0:T(8,128)(2,1)}, bf16[2,2304,128]{2,1,0:T(8,128)(2,1)S(1)}, u32[]{:S(2)}, u32[]{:S(2)}) collective-permute-start(bf16[2,2304,128]{2,1,0:T(8,128)(2,1)} %get-tuple-element.428), channel_id=1, source_target_pairs={{0,32},{8,40},{16,48},{24,56},{32,64},{40,72},{48,80},{56,88},{64,... | collective-permute-start | bytes 3538952 | tf_op jit(solution)/shard_map/while/body/eval_jaxpr/ppermute | solution.py:14
  280.5 4.2 copy-start.1
  283.2 1.8 copy-start.5
  285.0 1.2 copy-start.6
  298.8 32.5 %collective-permute-start = (bf16[2,2304,128]{2,1,0:T(8,128)(2,1)}, bf16[2,2304,128]{2,1,0:T(8,128)(2,1)S(1)}, u32[]{:S(2)}, u32[]{:S(2)}) collective-permute-start(bf16[2,2304,128]{2,1,0:T(8,128)(2,1)} %get-tuple-element.428), channel_id=1, source_target_pairs={{0,32},{8,40},{16,48},{24,56},{32,64},{40,72},{48,80},{56,88},{64,... | collective-permute-start | bytes 3538952 | tf_op jit(solution)/shard_map/while/body/eval_jaxpr/ppermute | solution.py:14
  333.3 4.2 copy-start.1
  336.0 1.8 copy-start.5
  351.5 33.0 %collective-permute-start = (bf16[2,2304,128]{2,1,0:T(8,128)(2,1)}, bf16[2,2304,128]{2,1,0:T(8,128)(2,1)S(1)}, u32[]{:S(2)}, u32[]{:S(2)}) collective-permute-start(bf16[2,2304,128]{2,1,0:T(8,128)(2,1)} %get-tuple-element.428), channel_id=1, source_target_pairs={{0,32},{8,40},{16,48},{24,56},{32,64},{40,72},{48,80},{56,88},{64,... | collective-permute-start | bytes 3538952 | tf_op jit(solution)/shard_map/while/body/eval_jaxpr/ppermute | solution.py:14
  386.6 4.2 copy-start.1
  389.3 1.8 copy-start.5
  391.1 1.2 copy-start.6
  404.8 32.3 %collective-permute-start = (bf16[2,2304,128]{2,1,0:T(8,128)(2,1)}, bf16[2,2304,128]{2,1,0:T(8,128)(2,1)S(1)}, u32[]{:S(2)}, u32[]{:S(2)}) collective-permute-start(bf16[2,2304,128]{2,1,0:T(8,128)(2,1)} %get-tuple-element.428), channel_id=1, source_target_pairs={{0,32},{8,40},{16,48},{24,56},{32,64},{40,72},{48,80},{56,88},{64,... | collective-permute-start | bytes 3538952 | tf_op jit(solution)/shard_map/while/body/eval_jaxpr/ppermute | solution.py:14
  439.2 4.2 copy-start.1
  441.9 1.8 copy-start.5
  (5 other events, 5.3 us)
Sparse Core Ops, SparseCore 0:
  10.6 30.1 all-gather.1
  461.8 169.4 all-reduce.1
where the time goes:
time: 642 us; the launch traced here: 640 us
  waiting for transfers between devices  399 us (62%)
  matrix products  84.8 us (13%)
  local copies, waits for them, and re-layouts  67 us (10%)
  other arithmetic  48 us (7%)
  starting transfers between devices  25.4 us (4%)
  between operations  15.5 us (2%)
    ppermute x7, waiting for transfers between devices, shifted(): lax.ppermute(shard, axis, [(i, (i + by) % devices) for i in range(devices)])  205 us
    psum x1, waiting for transfers between devices, shards(): lax.psum(partial_value.astype(jnp.bfloat16), 'head').astype(jnp.float32)  170 us
    dot_general x16, matrix products, attend(): jnp.einsum('gqk,kgd->gqd', weights.astype(jnp.bfloat16), value_block.resh...  46.8 us
    dot_general x16, matrix products, attend(): jnp.einsum('gqd,kgd->gqk', query_group, key_block.reshape(-1, kv_heads, H...  27.8 us
    scatter x8, local copies, waits for them, and re-layouts, write_fresh(): out_keys = out_keys.at[target].set(fresh_keys, mode='drop')  25.5 us
    scatter x8, local copies, waits for them, and re-layouts, write_fresh(): out_values = out_values.at[target].set(fresh_values, mode='drop')  25.5 us
    ppermute x7, starting transfers between devices, shifted(): lax.ppermute(shard, axis, [(i, (i + by) % devices) for i in range(devices)])  25.3 us
    all_gather x1, waiting for transfers between devices, shards(): gathered = lax.all_gather(tokens, 'head', axis=1, tiled=True)  23.6 us
  transfers between devices with their start and end apart: 9, of which 9 were waited for; matrix products, arithmetic and copies ran while one was open for 3% of the time, Pallas kernels for 0%

commit v1 on v0

--- a/solution.py
+++ b/solution.py
@@ -189,7 +189,9 @@
         .astype(jnp.bfloat16)
     )
     partial_value = jnp.dot(attended, w_out, preferred_element_type=jnp.float32)
-    summed = lax.psum(partial_value.astype(jnp.bfloat16), "head").astype(jnp.float32)
+    summed = jnp.sum(
+        lax.all_gather(partial_value.astype(jnp.bfloat16), axis_name="head"), axis=0
+    ).astype(jnp.float32)
     share_width = partial_value.shape[1] // lax.axis_size("head")
     projected = lax.dynamic_slice_in_dim(
         summed, lax.axis_index("head") * share_width, share_width, 1

time: 642 us -> 652 us (1.016)
  other arithmetic: 48 us -> 56.8 us
    all_gather x0 -> x1, waiting for transfers between devices: none -> 170 us  [shards(): lax.all_gather(partial_value.astype(jnp.bfloat16), axis_name='head')]
    psum x1 -> x0, waiting for transfers between devices: 170 us -> none  [shards(): lax.psum(partial_value.astype(jnp.bfloat16), 'head').astype(jnp.float32)]
    reduce_sum x0 -> x1, other arithmetic: none -> 8.77 us  [shards(): jnp.sum(lax.all_gather(partial_value.astype(jnp.bfloat16), axis_name='hea...]
where the time goes in v1:
time: 652 us; the launch traced here: 648 us
  waiting for transfers between devices  399 us (61%)
  matrix products  84.8 us (13%)
  local copies, waits for them, and re-layouts  66 us (10%)
  other arithmetic  56.8 us (9%)
  starting transfers between devices  25.6 us (4%)
  between operations  15.6 us (2%)
    ppermute x7, waiting for transfers between devices, shifted(): lax.ppermute(shard, axis, [(i, (i + by) % devices) for i in range(devices)])  205 us
    all_gather x1, waiting for transfers between devices, shards(): lax.all_gather(partial_value.astype(jnp.bfloat16), axis_name='head')  170 us
    dot_general x16, matrix products, attend(): jnp.einsum('gqk,kgd->gqd', weights.astype(jnp.bfloat16), value_block.resh...  46.8 us
    dot_general x16, matrix products, attend(): jnp.einsum('gqd,kgd->gqk', query_group, key_block.reshape(-1, kv_heads, H...  27.8 us
    scatter x8, local copies, waits for them, and re-layouts, write_fresh(): out_values = out_values.at[target].set(fresh_values, mode='drop')  25.5 us
    ppermute x7, starting transfers between devices, shifted(): lax.ppermute(shard, axis, [(i, (i + by) % devices) for i in range(devices)])  25.5 us
    scatter x8, local copies, waits for them, and re-layouts, write_fresh(): out_keys = out_keys.at[target].set(fresh_keys, mode='drop')  24 us
    all_gather x1, waiting for transfers between devices, shards(): gathered = lax.all_gather(tokens, 'head', axis=1, tiled=True)  23.6 us
  transfers between devices with their start and end apart: 9, of which 9 were waited for; matrix products, arithmetic and copies ran while one was open for 3% of the time, Pallas kernels for 0%

profile of v1, /device:TPU:2, one launch (start us, length us, event | category | flops | bytes accessed | tf_op | source)
XLA Modules:
  0.0 648.4 jit_solution(15483770678290170352)
XLA Ops:
  17.1 23.6 %all-gather.4.cloned.1.call-done = bf16[256,3072]{1,0:T(8,128)(2,1)} async-done(((bf16[256,384]{1,0:T(8,128)(2,1)}), bf16[256,3072]{1,0:T(8,128)(2,1)}) %all-gather.4.cloned.1.call-update) | async-done | bytes 1572880 | tf_op jit(solution)/shard_map/all_gather | solution.py:46
  51.8 3.2 scatter_custom_fusion.3
  56.1 3.3 fusion.81
  70.4 386.1 %while.25 = (s32[]{:T(128)}, bf16[2,2304,128]{2,1,0:T(8,128)(2,1)}, f32[1,768]{1,0:T(1,128)S(1)}, f32[1,768]{1,0:T(1,128)}, f32[1,768,128]{2,1,0:T(8,128)}, /*in...) while((s32[]{:T(128)}, bf16[2,2304,128]{2,1,0:T(8,128)(2,1)}, ...), condition=%wide.region_14.15_spmd, body=%wide.region_7.14_spmd.sunk | while | flops 929181184 | bytes 57951692 | solution.py:181
  70.4 5.7 collective-permute-start
  78.0 41.6 %collective-permute-done = bf16[2,2304,128]{2,1,0:T(8,128)(2,1)S(1)} collective-permute-done((bf16[2,2304,128]{2,1,0:T(8,128)(2,1)}, bf16[2,2304,128]{2,1,0:T(8,128)(2,1)S(1)}, u32[]{:S(2)}, u32[]{:S(2)}) %collective-permute-start) | collective-permute-done | bytes 1179680 | tf_op jit(solution)/shard_map/while/body/eval_jaxpr/ppermute | solution.py:14
  128.4 3.2 scatter_custom_fusion.15
  131.6 3.2 scatter_custom_fusion.14
  134.8 5.2 fusion.109
  140.0 5.2 collective-permute-start
  147.0 23.2 %collective-permute-done = bf16[2,2304,128]{2,1,0:T(8,128)(2,1)S(1)} collective-permute-done((bf16[2,2304,128]{2,1,0:T(8,128)(2,1)}, bf16[2,2304,128]{2,1,0:T(8,128)(2,1)S(1)}, u32[]{:S(2)}, u32[]{:S(2)}) %collective-permute-start) | collective-permute-done | bytes 1179680 | tf_op jit(solution)/shard_map/while/body/eval_jaxpr/ppermute | solution.py:14
  179.0 3.2 scatter_custom_fusion.15
  185.3 5.2 fusion.109
  190.5 4.3 collective-permute-start
  196.7 27.7 %collective-permute-done = bf16[2,2304,128]{2,1,0:T(8,128)(2,1)S(1)} collective-permute-done((bf16[2,2304,128]{2,1,0:T(8,128)(2,1)}, bf16[2,2304,128]{2,1,0:T(8,128)(2,1)S(1)}, u32[]{:S(2)}, u32[]{:S(2)}) %collective-permute-start) | collective-permute-done | bytes 1179680 | tf_op jit(solution)/shard_map/while/body/eval_jaxpr/ppermute | solution.py:14
  233.1 3.2 scatter_custom_fusion.15
  239.5 5.2 fusion.109
  248.1 29.3 %collective-permute-done = bf16[2,2304,128]{2,1,0:T(8,128)(2,1)S(1)} collective-permute-done((bf16[2,2304,128]{2,1,0:T(8,128)(2,1)}, bf16[2,2304,128]{2,1,0:T(8,128)(2,1)S(1)}, u32[]{:S(2)}, u32[]{:S(2)}) %collective-permute-start) | collective-permute-done | bytes 1179680 | tf_op jit(solution)/shard_map/while/body/eval_jaxpr/ppermute | solution.py:14
  286.2 3.2 scatter_custom_fusion.15
  292.6 5.2 fusion.109
  302.5 27.7 %collective-permute-done = bf16[2,2304,128]{2,1,0:T(8,128)(2,1)S(1)} collective-permute-done((bf16[2,2304,128]{2,1,0:T(8,128)(2,1)}, bf16[2,2304,128]{2,1,0:T(8,128)(2,1)S(1)}, u32[]{:S(2)}, u32[]{:S(2)}) %collective-permute-start) | collective-permute-done | bytes 1179680 | tf_op jit(solution)/shard_map/while/body/eval_jaxpr/ppermute | solution.py:14
  339.0 3.2 scatter_custom_fusion.15
  345.4 5.2 fusion.109
  350.5 3.3 collective-permute-start
  355.7 27.8 %collective-permute-done = bf16[2,2304,128]{2,1,0:T(8,128)(2,1)S(1)} collective-permute-done((bf16[2,2304,128]{2,1,0:T(8,128)(2,1)}, bf16[2,2304,128]{2,1,0:T(8,128)(2,1)S(1)}, u32[]{:S(2)}, u32[]{:S(2)}) %collective-permute-start) | collective-permute-done | bytes 1179680 | tf_op jit(solution)/shard_map/while/body/eval_jaxpr/ppermute | solution.py:14
  392.3 3.2 scatter_custom_fusion.15
  398.7 5.2 fusion.109
  408.3 27.8 %collective-permute-done = bf16[2,2304,128]{2,1,0:T(8,128)(2,1)S(1)} collective-permute-done((bf16[2,2304,128]{2,1,0:T(8,128)(2,1)}, bf16[2,2304,128]{2,1,0:T(8,128)(2,1)S(1)}, u32[]{:S(2)}, u32[]{:S(2)}) %collective-permute-start) | collective-permute-done | bytes 1179680 | tf_op jit(solution)/shard_map/while/body/eval_jaxpr/ppermute | solution.py:14
  444.9 3.2 scatter_custom_fusion.15
  451.3 5.2 fusion.109
  460.7 170.4 %all-gather.6.cloned.1.call-done = bf16[2048,3072]{1,0:T(8,128)(2,1)} async-done(((bf16[256,3072]{1,0:T(8,128)(2,1)}), bf16[2048,3072]{1,0:T(8,128)(2,1)}) %all-gather.6.cloned.1.call-update) | async-done | bytes 12582928 | tf_op jit(solution)/shard_map/all_gather | solution.py:193
  631.2 8.8 %reduce_sum.74 = bf16[256,3072]{1,0:T(8,128)(2,1)} reduce(bf16[8,256,3072]{2,1,0:T(8,128)(2,1)} %bitcast.118, bf16[]{:T(256)} %constant.176.clone.1), dimensions={0}, to_apply=%region_15.16 | reduce | flops 5505024 | bytes 14155778 | tf_op jit(solution)/shard_map/reduce_sum | solution.py:192
  (212 shorter events, 137.8 us)
Async XLA Ops:
  7.2 451.3 %copy-start = (bf16[384,3072]{1,0:T(8,128)(2,1)S(1)}, bf16[384,3072]{1,0:T(8,128)(2,1)}, u32[]{:S(2)}) copy-start(bf16[384,3072]{1,0:T(8,128)(2,1)} %param.17) | copy-start | bytes 7077892
  7.2 35.9 %copy-start.9 = (f32[3072]{0:T(1024)S(1)}, f32[3072]{0:T(1024)}, u32[]{:S(2)}) copy-start(f32[3072]{0:T(1024)} %param.13) | copy-start | bytes 36868
  7.2 33.5 %all-gather.4.cloned.1.call-start = ((), (), s32[]{:S(2)}) async-start(), calls=%async_computation | async-start | bytes 1769472 | tf_op jit(solution)/shard_map/all_gather | solution.py:46
  10.3 620.8 %all-gather.6.cloned.1.call-start = ((), (), s32[]{:S(2)}) async-start(), calls=%async_computation.1 | async-start | bytes 14155776 | tf_op jit(solution)/shard_map/all_gather | solution.py:193
  48.4 7.7 %copy-start.8 = (f32[256]{0:T(256)S(1)}, f32[256]{0:T(256)}, u32[]{:S(2)}) copy-start(f32[256]{0:T(256)} %copy-done.7) | copy-start | bytes 3076
  56.1 3.4 copy-start.3
  56.1 3.4 copy-start.4
  70.4 49.2 %collective-permute-start = (bf16[2,2304,128]{2,1,0:T(8,128)(2,1)}, bf16[2,2304,128]{2,1,0:T(8,128)(2,1)S(1)}, u32[]{:S(2)}, u32[]{:S(2)}) collective-permute-start(bf16[2,2304,128]{2,1,0:T(8,128)(2,1)} %get-tuple-element.428), channel_id=1, source_target_pairs={{0,32},{8,40},{16,48},{24,56},{32,64},{40,72},{48,80},{56,88},{64,... | collective-permute-start | bytes 3538952 | tf_op jit(solution)/shard_map/while/body/eval_jaxpr/ppermute | solution.py:14
  121.7 4.5 copy-start.1
  124.6 1.6 copy-start.5
  126.2 2.2 copy-start.6
  140.0 30.2 %collective-permute-start = (bf16[2,2304,128]{2,1,0:T(8,128)(2,1)}, bf16[2,2304,128]{2,1,0:T(8,128)(2,1)S(1)}, u32[]{:S(2)}, u32[]{:S(2)}) collective-permute-start(bf16[2,2304,128]{2,1,0:T(8,128)(2,1)} %get-tuple-element.428), channel_id=1, source_target_pairs={{0,32},{8,40},{16,48},{24,56},{32,64},{40,72},{48,80},{56,88},{64,... | collective-permute-start | bytes 3538952 | tf_op jit(solution)/shard_map/while/body/eval_jaxpr/ppermute | solution.py:14
  172.3 4.5 copy-start.1
  175.1 1.6 copy-start.5
  176.8 2.2 copy-start.6
  190.5 33.8 %collective-permute-start = (bf16[2,2304,128]{2,1,0:T(8,128)(2,1)}, bf16[2,2304,128]{2,1,0:T(8,128)(2,1)S(1)}, u32[]{:S(2)}, u32[]{:S(2)}) collective-permute-start(bf16[2,2304,128]{2,1,0:T(8,128)(2,1)} %get-tuple-element.428), channel_id=1, source_target_pairs={{0,32},{8,40},{16,48},{24,56},{32,64},{40,72},{48,80},{56,88},{64,... | collective-permute-start | bytes 3538952 | tf_op jit(solution)/shard_map/while/body/eval_jaxpr/ppermute | solution.py:14
  226.4 4.5 copy-start.1
  230.9 2.2 copy-start.6
  244.7 32.8 %collective-permute-start = (bf16[2,2304,128]{2,1,0:T(8,128)(2,1)}, bf16[2,2304,128]{2,1,0:T(8,128)(2,1)S(1)}, u32[]{:S(2)}, u32[]{:S(2)}) collective-permute-start(bf16[2,2304,128]{2,1,0:T(8,128)(2,1)} %get-tuple-element.428), channel_id=1, source_target_pairs={{0,32},{8,40},{16,48},{24,56},{32,64},{40,72},{48,80},{56,88},{64,... | collective-permute-start | bytes 3538952 | tf_op jit(solution)/shard_map/while/body/eval_jaxpr/ppermute | solution.py:14
  279.5 4.5 copy-start.1
  284.0 2.2 copy-start.6
  297.8 32.4 %collective-permute-start = (bf16[2,2304,128]{2,1,0:T(8,128)(2,1)}, bf16[2,2304,128]{2,1,0:T(8,128)(2,1)S(1)}, u32[]{:S(2)}, u32[]{:S(2)}) collective-permute-start(bf16[2,2304,128]{2,1,0:T(8,128)(2,1)} %get-tuple-element.428), channel_id=1, source_target_pairs={{0,32},{8,40},{16,48},{24,56},{32,64},{40,72},{48,80},{56,88},{64,... | collective-permute-start | bytes 3538952 | tf_op jit(solution)/shard_map/while/body/eval_jaxpr/ppermute | solution.py:14
  332.3 4.5 copy-start.1
  335.1 1.6 copy-start.5
  336.8 2.2 copy-start.6
  350.5 33.0 %collective-permute-start = (bf16[2,2304,128]{2,1,0:T(8,128)(2,1)}, bf16[2,2304,128]{2,1,0:T(8,128)(2,1)S(1)}, u32[]{:S(2)}, u32[]{:S(2)}) collective-permute-start(bf16[2,2304,128]{2,1,0:T(8,128)(2,1)} %get-tuple-element.428), channel_id=1, source_target_pairs={{0,32},{8,40},{16,48},{24,56},{32,64},{40,72},{48,80},{56,88},{64,... | collective-permute-start | bytes 3538952 | tf_op jit(solution)/shard_map/while/body/eval_jaxpr/ppermute | solution.py:14
  385.6 4.5 copy-start.1
  388.4 1.6 copy-start.5
  390.1 2.2 copy-start.6
  403.8 32.3 %collective-permute-start = (bf16[2,2304,128]{2,1,0:T(8,128)(2,1)}, bf16[2,2304,128]{2,1,0:T(8,128)(2,1)S(1)}, u32[]{:S(2)}, u32[]{:S(2)}) collective-permute-start(bf16[2,2304,128]{2,1,0:T(8,128)(2,1)} %get-tuple-element.428), channel_id=1, source_target_pairs={{0,32},{8,40},{16,48},{24,56},{32,64},{40,72},{48,80},{56,88},{64,... | collective-permute-start | bytes 3538952 | tf_op jit(solution)/shard_map/while/body/eval_jaxpr/ppermute | solution.py:14
  438.2 4.5 copy-start.1
  442.7 2.2 copy-start.6
  (5 other events, 6.2 us)
Sparse Core Ops, SparseCore 0:
  10.4 30.1 all-gather.3
  460.8 170.2 all-gather.5
